TPU v7x, 128 devices: a whole 4x4x4 slice. The times are simulated.
128 devices in a mesh: row: 8 (over y, core), col: 16 (over z, x).
Axes of the slice: x: 4, y: 4, z: 4, core: 2. Of those that a mesh axis runs over, the one named last changes fastest.
Arguments:
- child_fronts: float32 [2, 8192, 8192], P(None, 'row', 'col'), as said below
- parent_front: float32 [12288, 12288], P('row', 'col'), as said below
- child_map: int32 [2, 7168], replicated, may hold values from 0 to 12287, as said below
Outputs:
- child_factor: float32 [2, 8192, 1024], P(None, 'row', 'col')
- parent_factor: float32 [12288, 256], P('row', 'col')
- parent_schur: float32 [12288, 12288], P('row', 'col')
Inputs may be any that keep to these rules, and one draw needn't show every extreme that they name: child_fronts[k] and parent_front are symmetric positive definite. parent_front is symmetric positive definite. The entries of child_map[k] are distinct. Each aligned block of 512 entries of child_map[k] names exactly 32 indices in each aligned block of 768 parent indices.
All inputs are finite; a program needn't handle non-finite values.
Results may differ from a plain program's by a relative error of at most 0.0003.
Values sent between devices are 32-bit elements; how exact they have to be, the bound alone decides.
No kernel may reach another device: no remote copies, remote signals or barrier semaphores. Data moves between devices by JAX's collectives and lax.ppermute only.
A program may use at most 192 MiB of HBM per device.

v0:
```python
from functools import partial
import jax
import jax.numpy as jnp
from jax import lax
from jax.sharding import PartitionSpec as P

PP = 256
NB = 256
exact_mode = lax.Precision.HIGHEST


def from_root(value, axis, source):
    kept = jnp.where(lax.axis_index(axis) == source, value, 0).astype(value.dtype)
    return lax.psum(kept, axis)


def outer_update(factor_rows, crossed):
    return jnp.einsum("kin,kjn->kij", factor_rows, crossed, precision=exact_mode)


def take_rows(block, order):
    return jax.vmap(lambda single, picks: jnp.take(single, picks, axis=0))(block, order)


def take_both(block, row_order, col_order):
    rows_first = take_rows(block, row_order)
    flipped = take_rows(jnp.swapaxes(rows_first, 1, 2), col_order)
    return jnp.swapaxes(flipped, 1, 2)


def eliminate(tiles, pivots, send_panel, send_corner, send_cross):
    members, tile_rows, tile_cols = tiles.shape
    row_index = lax.axis_index("row")
    col_index = lax.axis_index("col")
    global_rows = row_index * tile_rows + jnp.arange(tile_rows, dtype=jnp.int32)
    total_steps = pivots // NB
    identity = jnp.broadcast_to(jnp.eye(NB, dtype=jnp.float32), (members, NB, NB))
    collected = []
    current = send_panel(lax.slice_in_dim(tiles, 0, NB, axis=2), 0)
    for panel_step in range(total_steps):
        offset = panel_step * NB
        owner_row = offset // tile_rows
        within_row = offset - owner_row * tile_rows
        corner = send_corner(
            lax.slice_in_dim(current, within_row, within_row + NB, axis=1), owner_row
        )
        factor = jnp.linalg.cholesky(corner)
        inverse = jax.vmap(partial(jax.scipy.linalg.solve_triangular, lower=True))(factor, identity)
        solved = jnp.einsum("krn,kmn->krm", current, inverse, precision=exact_mode)
        factor_rows = jnp.where((global_rows >= offset)[None, :, None], solved, jnp.float32(0.0))
        cross_first = col_index * tile_cols
        cross_owner = cross_first // tile_rows
        local_first = jnp.clip(cross_first - row_index * tile_rows, 0, tile_rows - tile_cols)
        crossed = send_cross(
            lax.dynamic_slice_in_dim(factor_rows, local_first, tile_cols, axis=1), cross_owner
        )
        collected.append(factor_rows)
        if panel_step + 1 < total_steps:
            upcoming = offset + NB
            next_owner = upcoming // tile_cols
            next_within = upcoming - next_owner * tile_cols
            tiles = tiles - outer_update(factor_rows, crossed)
            current = send_panel(
                lax.slice_in_dim(tiles, next_within, next_within + NB, axis=2), next_owner
            )
        else:
            tiles = tiles - outer_update(factor_rows, crossed)
    return (tiles, jnp.concatenate(collected, axis=2))


def inverse_list(targets, length, filler):
    sources = jnp.arange(targets.shape[0], dtype=jnp.int32)
    start = jnp.full((length,), filler, jnp.int32)
    return start.at[targets].set(sources, mode="drop")


def extend_add(tiles, child_map, parent_front):
    members, tile_rows, tile_cols = tiles.shape
    row_count = lax.axis_size("row")
    col_count = lax.axis_size("col")
    row_index = lax.axis_index("row")
    col_index = lax.axis_index("col")
    width = tile_rows * row_count
    pivots = width - child_map.shape[1]
    parent_rows = parent_front.shape[0]
    parent_cols = parent_front.shape[1]
    row_slots = tile_rows // row_count
    col_slots = tile_cols // col_count
    full_map = jnp.concatenate([jnp.zeros((members, pivots), jnp.int32), child_map], axis=1)
    positions = jnp.arange(width, dtype=jnp.int32)[None, :]
    row_keys = jnp.where(positions < pivots, row_count, full_map // parent_rows)
    col_keys = jnp.where(positions < pivots, col_count, full_map // parent_cols)
    row_orders = jnp.argsort(row_keys.reshape(members, row_count, tile_rows), axis=2, stable=True)
    col_orders = jnp.argsort(col_keys.reshape(members, col_count, tile_cols), axis=2, stable=True)
    row_blocks = jnp.arange(row_count, dtype=jnp.int32)
    col_blocks = jnp.arange(col_count, dtype=jnp.int32)
    row_live = jnp.clip((row_blocks + 1) * tile_rows - pivots, 0, tile_rows) // row_count
    col_live = jnp.clip((col_blocks + 1) * tile_cols - pivots, 0, tile_cols) // col_count
    row_seats = jnp.arange(row_slots, dtype=jnp.int32)
    col_seats = jnp.arange(col_slots, dtype=jnp.int32)
    own_row_live = row_live[row_index]
    send_row_pos = jnp.minimum(
        row_blocks[:, None] * own_row_live + row_seats[None, :], tile_rows - 1
    )
    send_row_keep = jnp.broadcast_to(
        row_seats[None, :] < own_row_live, (row_count, row_slots)
    ).reshape(-1)
    own_row_order = jnp.take(row_orders, row_index, axis=1)
    send_rows = jnp.take(own_row_order, send_row_pos.reshape(-1), axis=1)
    own_col_live = col_live[col_index]
    send_col_pos = jnp.minimum(
        col_blocks[:, None] * own_col_live + col_seats[None, :], tile_cols - 1
    )
    send_col_keep = jnp.broadcast_to(
        col_seats[None, :] < own_col_live, (col_count, col_slots)
    ).reshape(-1)
    own_col_order = jnp.take(col_orders, col_index, axis=1)
    send_cols = jnp.take(own_col_order, send_col_pos.reshape(-1), axis=1)
    picked = take_both(tiles, send_rows, send_cols)
    picked = jnp.where(
        send_row_keep[None, :, None] & send_col_keep[None, None, :], picked, jnp.float32(0.0)
    )
    outgoing = jnp.transpose(
        picked.reshape(members, row_count, row_slots, col_count, col_slots), (1, 3, 0, 2, 4)
    )
    flat = outgoing.reshape(row_count * col_count, members, row_slots, col_slots)
    arrived = lax.all_to_all(flat, ("row", "col"), split_axis=0, concat_axis=0, tiled=True)
    arrived = arrived.reshape(row_count, col_count, members, row_slots, col_slots)
    received = jnp.transpose(arrived, (2, 0, 3, 1, 4)).reshape(members, tile_rows, tile_cols)
    recv_row_pos = jnp.minimum(row_index * row_live[:, None] + row_seats[None, :], tile_rows - 1)
    recv_row_keep = (row_seats[None, :] < row_live[:, None]).reshape(-1)
    local_rows = jnp.take_along_axis(row_orders, recv_row_pos[None, :, :], axis=2)
    global_rows = (row_blocks[None, :, None] * tile_rows + local_rows).reshape(members, -1)
    target_rows = jnp.take_along_axis(full_map, global_rows, axis=1) - row_index * parent_rows
    target_rows = jnp.where(recv_row_keep[None, :], target_rows, parent_rows)
    recv_col_pos = jnp.minimum(col_index * col_live[:, None] + col_seats[None, :], tile_cols - 1)
    recv_col_keep = (col_seats[None, :] < col_live[:, None]).reshape(-1)
    local_cols = jnp.take_along_axis(col_orders, recv_col_pos[None, :, :], axis=2)
    global_cols = (col_blocks[None, :, None] * tile_cols + local_cols).reshape(members, -1)
    target_cols = jnp.take_along_axis(full_map, global_cols, axis=1) - col_index * parent_cols
    target_cols = jnp.where(recv_col_keep[None, :], target_cols, parent_cols)
    row_sources = jax.vmap(lambda targets: inverse_list(targets, parent_rows, tile_rows))(
        target_rows
    )
    col_sources = jax.vmap(lambda targets: inverse_list(targets, parent_cols, tile_cols))(
        target_cols
    )
    padded = jnp.concatenate([received, jnp.zeros((members, 1, tile_cols), jnp.float32)], axis=1)
    placed_rows = take_rows(padded, row_sources)
    flipped = jnp.swapaxes(placed_rows, 1, 2)
    flipped = jnp.concatenate([flipped, jnp.zeros((members, 1, parent_rows), jnp.float32)], axis=1)
    placed = jnp.swapaxes(take_rows(flipped, col_sources), 1, 2)
    merged = parent_front
    for which_child in range(members):
        merged = merged + placed[which_child]
    return merged


def child_panel(piece, owner):
    return from_root(piece, "col", owner)


def child_corner(piece, owner):
    return from_root(piece, "row", owner)


def child_cross(piece, owner):
    return from_root(piece, "row", owner)


def parent_panel(piece, owner):
    return from_root(piece, "col", owner)


def parent_corner(piece, owner):
    return from_root(piece, "row", owner)


def parent_cross(piece, owner):
    return from_root(piece, "row", owner)


def local(child_fronts, parent_front, child_map):
    col_count = lax.axis_size("col")
    row_index = lax.axis_index("row")
    col_index = lax.axis_index("col")
    tile_rows = child_fronts.shape[1]
    width = tile_rows * lax.axis_size("row")
    pivots = width - child_map.shape[1]
    updated, child_panels = eliminate(child_fronts, pivots, child_panel, child_corner, child_cross)
    merged = extend_add(updated, child_map, parent_front)
    parent_updated, parent_panels = eliminate(
        merged[None], PP, parent_panel, parent_corner, parent_cross
    )
    child_share = pivots // col_count
    child_factor = lax.dynamic_slice_in_dim(
        child_panels, col_index * child_share, child_share, axis=2
    )
    parent_share = PP // col_count
    parent_factor = lax.dynamic_slice_in_dim(
        parent_panels[0], col_index * parent_share, parent_share, axis=1
    )
    parent_rows = parent_front.shape[0]
    parent_cols = parent_front.shape[1]
    global_rows = row_index * parent_rows + jnp.arange(parent_rows, dtype=jnp.int32)
    global_cols = col_index * parent_cols + jnp.arange(parent_cols, dtype=jnp.int32)
    keep = (global_rows[:, None] >= PP) & (global_cols[None, :] >= PP)
    parent_schur = jnp.where(keep, parent_updated[0], jnp.float32(0.0))
    return (child_factor, parent_factor, parent_schur)


def solution(mesh):
    placed = (P(None, "row", "col"), P("row", "col"), P())
    return jax.shard_map(
        local,
        mesh=mesh,
        in_specs=placed,
        out_specs=(P(None, "row", "col"), P("row", "col"), P("row", "col")),
        check_vma=False,
    )
```

profile of v0, /device:TPU:0, one launch (start us, length us, event | category | flops | bytes accessed | tf_op | source)
XLA Modules:
  0.0 2048.3 jit_solution(9405431235240546591)
XLA Ops:
  16.8 92.8 %all-reduce.21.cloned.1.call-done = f32[2,1024,256]{1,2,0:T(8,128)} async-done(((f32[2,1024,256]{1,2,0:T(8,128)}), f32[2,1024,256]{1,2,0:T(8,128)}) %all-reduce.21.cloned.1.call-update) | async-done | bytes 2097168 | tf_op jit(solution)/shard_map/psum | solution.py:14
  111.5 61.1 %all-reduce.23.cloned.1.call-done = f32[2,256,256]{1,2,0:T(8,128)} async-done(((f32[2,256,256]{1,2,0:T(8,128)}), f32[2,256,256]{1,2,0:T(8,128)}) %all-reduce.23.cloned.1.call-update) | async-done | bytes 524304 | tf_op jit(solution)/shard_map/psum | solution.py:14
  175.0 23.5 %custom-call.62 = f32[2,128,128]{2,1,0:T(8,128)S(1)} custom-call(f32[2,128,128]{2,1,0:T(8,128)S(1)} %cholesky.464), custom_call_target="Cholesky" | custom-call | tf_op jit(solution)/shard_map/jit(cholesky)/cholesky | solution.py:47
  198.5 19.7 custom-call.63
  218.9 23.5 %custom-call.64 = f32[2,128,128]{2,1,0:T(8,128)S(1)} custom-call(f32[2,128,128]{2,1,0:T(8,128)S(1)} %convolution_subtract_fusion.11), custom_call_target="Cholesky" | custom-call | tf_op jit(solution)/shard_map/jit(cholesky)/cholesky | solution.py:47
  246.8 39.5 %custom-call.65 = f32[2,2,128,128]{2,3,1,0:T(8,128)S(1)} custom-call(f32[2,2,128,128]{3,2,1,0:T(8,128)S(1)} %bitcast.389), custom_call_target="InvertDiagBlocksLowerTriangular" | custom-call | tf_op jit(solution)/shard_map/vmap(jit(_solve_triangular))/triangular_solve | solution.py:48
  292.8 61.7 %all-reduce.25.cloned.1.call-done = f32[2,512,256]{1,2,0:T(8,128)} async-done(((f32[2,512,256]{1,2,0:T(8,128)}), f32[2,512,256]{1,2,0:T(8,128)}) %all-reduce.25.cloned.1.call-update) | async-done | bytes 1048592 | tf_op jit(solution)/shard_map/psum | solution.py:14
  365.3 89.7 %all-reduce.27.cloned.1.call-done = f32[2,1024,256]{1,2,0:T(8,128)} async-done(((f32[2,1024,256]{1,2,0:T(8,128)}), f32[2,1024,256]{1,2,0:T(8,128)}) %all-reduce.27.cloned.1.call-update) | async-done | bytes 2097168 | tf_op jit(solution)/shard_map/psum | solution.py:14
  457.0 61.0 %all-reduce.29.cloned.1.call-done = f32[2,256,256]{1,2,0:T(8,128)} async-done(((f32[2,256,256]{1,2,0:T(8,128)}), f32[2,256,256]{1,2,0:T(8,128)}) %all-reduce.29.cloned.1.call-update) | async-done | bytes 524304 | tf_op jit(solution)/shard_map/psum | solution.py:14
  520.3 23.9 %custom-call.66 = f32[2,128,128]{2,1,0:T(8,128)S(1)} custom-call(f32[2,128,128]{2,1,0:T(8,128)S(1)} %cholesky.467), custom_call_target="Cholesky" | custom-call | tf_op jit(solution)/shard_map/jit(cholesky)/cholesky | solution.py:47
  544.2 19.7 custom-call.67
  564.6 23.5 %custom-call.68 = f32[2,128,128]{2,1,0:T(8,128)S(1)} custom-call(f32[2,128,128]{2,1,0:T(8,128)S(1)} %convolution_subtract_fusion.10), custom_call_target="Cholesky" | custom-call | tf_op jit(solution)/shard_map/jit(cholesky)/cholesky | solution.py:47
  592.5 39.5 %custom-call.69 = f32[2,2,128,128]{2,3,1,0:T(8,128)S(1)} custom-call(f32[2,2,128,128]{3,2,1,0:T(8,128)S(1)} %bitcast.390), custom_call_target="InvertDiagBlocksLowerTriangular" | custom-call | tf_op jit(solution)/shard_map/vmap(jit(_solve_triangular))/triangular_solve | solution.py:48
  638.6 61.7 %all-reduce.31.cloned.1.call-done = f32[2,512,256]{1,2,0:T(8,128)} async-done(((f32[2,512,256]{1,2,0:T(8,128)}), f32[2,512,256]{1,2,0:T(8,128)}) %all-reduce.31.cloned.1.call-update) | async-done | bytes 1048592 | tf_op jit(solution)/shard_map/psum | solution.py:14
  711.1 89.7 %all-reduce.33.cloned.1.call-done = f32[2,1024,256]{1,2,0:T(8,128)} async-done(((f32[2,1024,256]{1,2,0:T(8,128)}), f32[2,1024,256]{1,2,0:T(8,128)}) %all-reduce.33.cloned.1.call-update) | async-done | bytes 2097168 | tf_op jit(solution)/shard_map/psum | solution.py:14
  802.8 61.1 %all-reduce.35.cloned.1.call-done = f32[2,256,256]{1,2,0:T(8,128)} async-done(((f32[2,256,256]{1,2,0:T(8,128)}), f32[2,256,256]{1,2,0:T(8,128)}) %all-reduce.35.cloned.1.call-update) | async-done | bytes 524304 | tf_op jit(solution)/shard_map/psum | solution.py:14
  866.3 23.7 %custom-call.70 = f32[2,128,128]{2,1,0:T(8,128)S(1)} custom-call(f32[2,128,128]{2,1,0:T(8,128)S(1)} %cholesky.470), custom_call_target="Cholesky" | custom-call | tf_op jit(solution)/shard_map/jit(cholesky)/cholesky | solution.py:47
  890.0 19.7 custom-call.71
  910.4 23.5 %custom-call.72 = f32[2,128,128]{2,1,0:T(8,128)S(1)} custom-call(f32[2,128,128]{2,1,0:T(8,128)S(1)} %convolution_subtract_fusion.9), custom_call_target="Cholesky" | custom-call | tf_op jit(solution)/shard_map/jit(cholesky)/cholesky | solution.py:47
  938.3 39.7 %custom-call.73 = f32[2,2,128,128]{2,3,1,0:T(8,128)S(1)} custom-call(f32[2,2,128,128]{3,2,1,0:T(8,128)S(1)} %bitcast.391), custom_call_target="InvertDiagBlocksLowerTriangular" | custom-call | tf_op jit(solution)/shard_map/vmap(jit(_solve_triangular))/triangular_solve | solution.py:48
  991.8 54.5 %all-reduce.37.cloned.1.call-done = f32[2,512,256]{1,2,0:T(8,128)} async-done(((f32[2,512,256]{1,2,0:T(8,128)}), f32[2,512,256]{1,2,0:T(8,128)}) %all-reduce.37.cloned.1.call-update) | async-done | bytes 1048592 | tf_op jit(solution)/shard_map/psum | solution.py:14
  1072.1 74.7 %all-reduce.39.cloned.1.call-done = f32[2,1024,256]{1,2,0:T(8,128)} async-done(((f32[2,1024,256]{1,2,0:T(8,128)}), f32[2,1024,256]{1,2,0:T(8,128)}) %all-reduce.39.cloned.1.call-update) | async-done | bytes 2097168 | tf_op jit(solution)/shard_map/psum | solution.py:14
  1159.9 50.0 %all-reduce.41.cloned.1.call-done = f32[2,256,256]{1,2,0:T(8,128)} async-done(((f32[2,256,256]{1,2,0:T(8,128)}), f32[2,256,256]{1,2,0:T(8,128)}) %all-reduce.41.cloned.1.call-update) | async-done | bytes 524304 | tf_op jit(solution)/shard_map/psum | solution.py:14
  1212.3 23.5 %custom-call.74 = f32[2,128,128]{2,1,0:T(8,128)S(1)} custom-call(f32[2,128,128]{2,1,0:T(8,128)S(1)} %cholesky.473), custom_call_target="Cholesky" | custom-call | tf_op jit(solution)/shard_map/jit(cholesky)/cholesky | solution.py:47
  1235.8 19.7 custom-call.75
  1256.2 23.5 %custom-call.76 = f32[2,128,128]{2,1,0:T(8,128)S(1)} custom-call(f32[2,128,128]{2,1,0:T(8,128)S(1)} %convolution_subtract_fusion.8), custom_call_target="Cholesky" | custom-call | tf_op jit(solution)/shard_map/jit(cholesky)/cholesky | solution.py:47
  1284.1 39.5 %custom-call.77 = f32[2,2,128,128]{2,3,1,0:T(8,128)S(1)} custom-call(f32[2,2,128,128]{3,2,1,0:T(8,128)S(1)} %bitcast.392), custom_call_target="InvertDiagBlocksLowerTriangular" | custom-call | tf_op jit(solution)/shard_map/vmap(jit(_solve_triangular))/triangular_solve | solution.py:48
  1330.3 61.7 %all-reduce.43.cloned.1.call-done = f32[2,512,256]{1,2,0:T(8,128)} async-done(((f32[2,512,256]{1,2,0:T(8,128)}), f32[2,512,256]{1,2,0:T(8,128)}) %all-reduce.43.cloned.1.call-update) | async-done | bytes 1048592 | tf_op jit(solution)/shard_map/psum | solution.py:14
  1404.4 35.7 %gather_fusion.6 = f32[2048,512]{1,0:T(8,128)} fusion(f32[2,1024,512]{2,1,0:T(8,128)} %copy.472, s32[2048]{0:T(1024)S(1)} %bitcast.375), kind=kCustom, calls=%fused_computation.6 | custom fusion | bytes 8404992 | tf_op jit(solution)/shard_map/vmap(jit(_take))/gather | solution.py:22
  1450.5 20.9 %gather_fusion.7 = f32[1024,1024]{1,0:T(8,128)} fusion(f32[2,512,1024]{2,1,0:T(8,128)} %select_bitcast_fusion.2, s32[1024]{0:T(1024)S(1)} %bitcast.377), kind=kCustom, calls=%fused_computation.7 | custom fusion | bytes 8396800 | tf_op jit(solution)/shard_map/vmap(jit(_take))/gather | solution.py:22
  1477.9 8.6 all-to-all-start
  1486.8 10.5 gather_fusion.4
  1497.6 17.7 gather_fusion.5
  1516.4 8.1 scatter_custom_fusion.1
  1524.6 9.1 gather_fusion.3
  1538.9 7.9 copy.475
  1564.5 85.5 %gather_fusion.8 = f32[3072,512]{1,0:T(8,128)} fusion(f32[2,1025,512]{2,0,1:T(2,128)} %concatenate.19, s32[3072]{0:T(1024)S(1)} %reshape.1289), kind=kCustom, calls=%fused_computation.8 | custom fusion | bytes 12607488 | tf_op jit(solution)/shard_map/vmap(jit(_take))/gather | solution.py:22
  1650.1 10.4 copy.477
  1660.5 8.1 select_bitcast_fusion.1
  1676.2 51.1 %gather_fusion.9 = f32[1536,1536]{1,0:T(8,128)} fusion(f32[2,513,1536]{2,0,1:T(2,128)} %concatenate.20, s32[1536]{0:T(1024)S(1)} %reshape.1295), kind=kCustom, calls=%fused_computation.9 | custom fusion | bytes 18886656 | tf_op jit(solution)/shard_map/vmap(jit(_take))/gather | solution.py:22
  1740.4 89.8 %all-reduce.45.cloned.1.call-done = f32[1,1536,256]{1,2,0:T(8,128)} async-done(((f32[1,1536,256]{1,2,0:T(8,128)}), f32[1,1536,256]{1,2,0:T(8,128)}) %all-reduce.45.cloned.1.call-update) | async-done | bytes 1572880 | tf_op jit(solution)/shard_map/psum | solution.py:14
  1832.2 59.8 %all-reduce.47.cloned.1.call-done = f32[1,256,256]{1,2,0:T(8,128)} async-done(((f32[1,256,256]{1,2,0:T(8,128)}), f32[1,256,256]{1,2,0:T(8,128)}) %all-reduce.47.cloned.1.call-update) | async-done | bytes 262160 | tf_op jit(solution)/shard_map/psum | solution.py:14
  1894.1 11.7 custom-call.30
  1906.0 9.8 custom-call.31
  1916.4 11.7 custom-call.32
  1935.0 19.7 custom-call.33
  1963.7 58.2 %all-reduce.49.cloned.1.call-done = f32[768,256]{0,1:T(8,128)} async-done(((f32[768,256]{0,1:T(8,128)}), f32[768,256]{0,1:T(8,128)}) %all-reduce.49.cloned.1.call-update) | async-done | bytes 786448 | tf_op jit(solution)/shard_map/psum | solution.py:14
  2021.9 12.7 subtract_select_fusion
  (346 shorter events, 257.4 us)
Async XLA Ops:
  8.0 101.5 %all-reduce.21.cloned.1.call-start = ((), (), s32[]{:S(2)}) async-start(), calls=%async_computation.1 | async-start | bytes 4194304 | tf_op jit(solution)/shard_map/psum | solution.py:14
  16.6 156.0 %all-reduce.23.cloned.1.call-start = ((), (), s32[]{:S(2)}) async-start(), calls=%async_computation.2 | async-start | bytes 1048576 | tf_op jit(solution)/shard_map/psum | solution.py:14
  111.4 243.1 %all-reduce.25.cloned.1.call-start = ((), (), s32[]{:S(2)}) async-start(), calls=%async_computation.3 | async-start | bytes 2097152 | tf_op jit(solution)/shard_map/psum | solution.py:14
  291.1 70.6 %copy-start.4 = (f32[2,1024,256]{1,2,0:T(8,128)}, f32[2,1024,256]{1,2,0:T(8,128)S(1)}, u32[]{:S(2)}) copy-start(f32[2,1024,256]{1,2,0:T(8,128)S(1)} %convolution_select_fusion.4) | copy-start | bytes 6291460
  292.7 162.3 %all-reduce.27.cloned.1.call-start = ((), (), s32[]{:S(2)}) async-start(), calls=%async_computation.4 | async-start | bytes 4194304 | tf_op jit(solution)/shard_map/psum | solution.py:14
  361.7 2.0 copy-start.3
  365.2 152.7 %all-reduce.29.cloned.1.call-start = ((), (), s32[]{:S(2)}) async-start(), calls=%async_computation.5 | async-start | bytes 1048576 | tf_op jit(solution)/shard_map/psum | solution.py:14
  456.9 243.4 %all-reduce.31.cloned.1.call-start = ((), (), s32[]{:S(2)}) async-start(), calls=%async_computation.6 | async-start | bytes 2097152 | tf_op jit(solution)/shard_map/psum | solution.py:14
  636.8 70.7 %copy-start.6 = (f32[2,1024,256]{1,2,0:T(8,128)}, f32[2,1024,256]{1,2,0:T(8,128)S(1)}, u32[]{:S(2)}) copy-start(f32[2,1024,256]{1,2,0:T(8,128)S(1)} %convolution_select_fusion.3) | copy-start | bytes 6291460
  638.5 162.3 %all-reduce.33.cloned.1.call-start = ((), (), s32[]{:S(2)}) async-start(), calls=%async_computation.7 | async-start | bytes 4194304 | tf_op jit(solution)/shard_map/psum | solution.py:14
  707.5 2.0 copy-start.2
  711.0 152.9 %all-reduce.35.cloned.1.call-start = ((), (), s32[]{:S(2)}) async-start(), calls=%async_computation.8 | async-start | bytes 1048576 | tf_op jit(solution)/shard_map/psum | solution.py:14
  802.7 243.6 %all-reduce.37.cloned.1.call-start = ((), (), s32[]{:S(2)}) async-start(), calls=%async_computation.9 | async-start | bytes 2097152 | tf_op jit(solution)/shard_map/psum | solution.py:14
  982.8 70.7 %copy-start.7 = (f32[2,1024,256]{1,2,0:T(8,128)}, f32[2,1024,256]{1,2,0:T(8,128)S(1)}, u32[]{:S(2)}) copy-start(f32[2,1024,256]{1,2,0:T(8,128)S(1)} %convolution_select_fusion.2) | copy-start | bytes 6291460
  982.8 1.7 copy-start.10
  984.5 79.8 %sort.39.cloned.1.call-start = ((), (), s32[]{:S(2)}) async-start(), calls=%async_computation.17 | async-start | bytes 393248 | tf_op jit(solution)/shard_map/jit(argsort)/sort | solution.py:93
  986.2 81.5 %sort.37.cloned.1.call-start = ((), (), s32[]{:S(2)}) async-start(), calls=%async_computation.16 | async-start | bytes 393248 | tf_op jit(solution)/shard_map/jit(argsort)/sort | solution.py:94
  987.5 159.3 %all-reduce.39.cloned.1.call-start = ((), (), s32[]{:S(2)}) async-start(), calls=%async_computation.10 | async-start | bytes 4194304 | tf_op jit(solution)/shard_map/psum | solution.py:14
  1053.5 2.0 copy-start.1
  1057.0 152.9 %all-reduce.41.cloned.1.call-start = ((), (), s32[]{:S(2)}) async-start(), calls=%async_computation.11 | async-start | bytes 1048576 | tf_op jit(solution)/shard_map/psum | solution.py:14
  1148.7 243.2 %all-reduce.43.cloned.1.call-start = ((), (), s32[]{:S(2)}) async-start(), calls=%async_computation.12 | async-start | bytes 2097152 | tf_op jit(solution)/shard_map/psum | solution.py:14
  1328.5 70.4 %copy-start.8 = (f32[2,1024,256]{1,2,0:T(8,128)}, f32[2,1024,256]{1,2,0:T(8,128)S(1)}, u32[]{:S(2)}) copy-start(f32[2,1024,256]{1,2,0:T(8,128)S(1)} %convolution_select_fusion.1) | copy-start | bytes 6291460
  1477.9 61.1 %all-to-all-start = ((f32[128,2,128,32]{2,3,1,0:T(8,128)}), f32[128,2,128,32]{2,3,1,0:T(8,128)}, u32[]{:S(2)}, u32[]{:S(2)}) async-start(f32[128,2,128,32]{2,3,1,0:T(8,128)} %bitcast.384), calls=%async_computation | async-start | bytes 8388608 | tf_op jit(solution)/shard_map/all_to_all | solution.py:127
  1486.5 343.7 %all-reduce.45.cloned.1.call-start = ((), (), s32[]{:S(2)}) async-start(), calls=%async_computation.13 | async-start | bytes 3145728 | tf_op jit(solution)/shard_map/psum | solution.py:14
  1497.6 17.8 copy-start.14
  1497.6 18.2 copy-start.12
  1524.6 9.2 copy-start.13
  1524.6 9.5 copy-start.11
  1731.7 7.4 copy-start
  1740.3 151.7 %all-reduce.47.cloned.1.call-start = ((), (), s32[]{:S(2)}) async-start(), calls=%async_computation.14 | async-start | bytes 524288 | tf_op jit(solution)/shard_map/psum | solution.py:14
  1831.9 190.0 %all-reduce.49.cloned.1.call-start = ((), (), s32[]{:S(2)}) async-start(), calls=%async_computation.15 | async-start | bytes 1572864 | tf_op jit(solution)/shard_map/psum | solution.py:14
  1955.6 5.5 copy-start.5
  1958.7 1.1 copy-start.9
Sparse Core Ops, SparseCore 0:
  16.7 92.7 all-reduce.20
  112.6 60.0 all-reduce.22
  292.9 61.5 all-reduce.24
  365.4 89.5 all-reduce.26
  457.9 60.0 all-reduce.28
  638.7 61.5 all-reduce.30
  711.2 89.6 all-reduce.32
  803.8 60.0 all-reduce.34
  984.6 61.6 all-reduce.36
  1057.1 89.6 all-reduce.38
  1149.8 60.0 all-reduce.40
  1330.3 61.5 all-reduce.42
  1740.4 89.7 all-reduce.44
  1832.9 59.0 all-reduce.46
  1961.2 60.7 all-reduce.48
Sparse Core Ops, SparseCore 1:
  988.0 6.9 sort.43.cloned.1.call-done
  997.5 9.8 sort.41.cloned.1.call-done
  (2 shorter events, 0.0 us)
where the time goes:
time: 2060 us; the launch traced here: 2050 us
  waiting for transfers between devices  1030 us (50%)
  other arithmetic  548 us (27%)
  local copies, waits for them, and re-layouts  377 us (18%)
  matrix products  67.7 us (3%)
    psum x15, waiting for transfers between devices, from_root(): return lax.psum(kept, axis)  1030 us
    another operation x40, other arithmetic, eliminate(): factor = jnp.linalg.cholesky(corner)  303 us
    gather x8, local copies, waits for them, and re-layouts, take_rows(): jnp.take(single, picks, axis=0)  209 us
    another operation x12, other arithmetic, eliminate(): jax.vmap(partial(jax.scipy.linalg.solve_triangular, lower=True))  179 us
    dot_general x5, matrix products, outer_update(): jnp.einsum('kin,kjn->kij', factor_rows, crossed, precision=exact_mode)  41.4 us
  transfers between devices with their start and end apart: 16, of which 15 were waited for; matrix products, arithmetic and copies ran while one was open for 4% of the time, Pallas kernels for 0%

commit v1 on v0

--- a/solution.py
+++ b/solution.py
@@ -11,7 +11,7 @@
 
 def from_root(value, axis, source):
     kept = jnp.where(lax.axis_index(axis) == source, value, 0).astype(value.dtype)
-    return lax.psum(kept, axis)
+    return jnp.sum(lax.all_gather(kept, axis), axis=0)
 
 
 def outer_update(factor_rows, crossed):

time: 2060 us -> 2420 us (1.17)
  waiting for transfers between devices: 1030 us -> 1300 us
  other arithmetic: 548 us -> 613 us
    all_gather x0 -> x15, waiting for transfers between devices: none -> 1290 us  [from_root(): return jnp.sum(lax.all_gather(kept, axis), axis=0)]
    psum x15 -> x0, waiting for transfers between devices: 1030 us -> none  [from_root(): return lax.psum(kept, axis)]
    unnamed x10 -> x19, other arithmetic: 0.55 us -> 65.2 us
    gather x8 -> x9, local copies, waits for them, and re-layouts: 209 us -> 219 us  [take_rows(): jnp.take(single, picks, axis=0)]
  transfers between devices with their start and end apart: 16 -> 16, of which waited for: 15 -> 16; matrix products, arithmetic and copies ran while one was open for 4% -> 3% of each run, Pallas kernels for 0% -> 0%
where the time goes in v1:
time: 2420 us; the launch traced here: 2400 us
  waiting for transfers between devices  1300 us (54%)
  other arithmetic  613 us (25%)
  local copies, waits for them, and re-layouts  397 us (16%)
  matrix products  58 us (2%)
    all_gather x15, waiting for transfers between devices, from_root(): return jnp.sum(lax.all_gather(kept, axis), axis=0)  1290 us
    another operation x40, other arithmetic, eliminate(): factor = jnp.linalg.cholesky(corner)  303 us
    gather x9, local copies, waits for them, and re-layouts, take_rows(): jnp.take(single, picks, axis=0)  219 us
    another operation x12, other arithmetic, eliminate(): jax.vmap(partial(jax.scipy.linalg.solve_triangular, lower=True))  179 us
    unnamed x19, other arithmetic  65.2 us
  transfers between devices with their start and end apart: 16, of which 16 were waited for; matrix products, arithmetic and copies ran while one was open for 3% of the time, Pallas kernels for 0%

profile of v1, /device:TPU:0, one launch (start us, length us, event | category | flops | bytes accessed | tf_op | source)
XLA Modules:
  0.0 2400.5 jit_solution(12774446542400674242)
XLA Ops:
  17.1 199.8 %all-gather.31.cloned.1.call-done = f32[32,1024,256]{2,1,0:T(8,128)} async-done(((f32[2,1024,256]{2,1,0:T(8,128)}), f32[32,1024,256]{2,1,0:T(8,128)}) %all-gather.31.cloned.1.call-update) | async-done | bytes 33554448 | tf_op jit(solution)/shard_map/all_gather | solution.py:14
  216.9 12.1 reduce_sum.139
  230.7 31.7 %all-gather.33.cloned.1.call-done = f32[16,256,256]{2,1,0:T(8,128)} async-done(((f32[2,256,256]{2,1,0:T(8,128)}), f32[16,256,256]{2,1,0:T(8,128)}) %all-gather.33.cloned.1.call-update) | async-done | bytes 4194320 | tf_op jit(solution)/shard_map/all_gather | solution.py:14
  265.2 23.5 custom-call.62
  288.7 19.7 custom-call.63
  309.1 23.5 custom-call.64
  337.1 39.5 %custom-call.65 = f32[2,2,128,128]{2,3,1,0:T(8,128)S(1)} custom-call(f32[2,2,128,128]{3,2,1,0:T(8,128)S(1)} %bitcast.432), custom_call_target="InvertDiagBlocksLowerTriangular" | custom-call | tf_op jit(solution)/shard_map/vmap(jit(_solve_triangular))/triangular_solve | solution.py:48
  383.3 49.8 %all-gather.35.cloned.1.call-done = f32[16,512,256]{2,1,0:T(8,128)} async-done(((f32[2,512,256]{2,1,0:T(8,128)}), f32[16,512,256]{2,1,0:T(8,128)}) %all-gather.35.cloned.1.call-update) | async-done | bytes 8388624 | tf_op jit(solution)/shard_map/all_gather | solution.py:14
  446.8 197.5 %all-gather.37.cloned.1.call-done = f32[32,1024,256]{2,1,0:T(8,128)} async-done(((f32[2,1024,256]{2,1,0:T(8,128)}), f32[32,1024,256]{2,1,0:T(8,128)}) %all-gather.37.cloned.1.call-update) | async-done | bytes 33554448 | tf_op jit(solution)/shard_map/all_gather | solution.py:14
  644.2 12.1 reduce_sum.142
  657.9 31.8 %all-gather.39.cloned.1.call-done = f32[16,256,256]{2,1,0:T(8,128)} async-done(((f32[2,256,256]{2,1,0:T(8,128)}), f32[16,256,256]{2,1,0:T(8,128)}) %all-gather.39.cloned.1.call-update) | async-done | bytes 4194320 | tf_op jit(solution)/shard_map/all_gather | solution.py:14
  692.6 23.7 custom-call.66
  716.3 19.7 custom-call.67
  736.7 23.5 custom-call.68
  764.7 39.7 %custom-call.69 = f32[2,2,128,128]{2,3,1,0:T(8,128)S(1)} custom-call(f32[2,2,128,128]{3,2,1,0:T(8,128)S(1)} %bitcast.433), custom_call_target="InvertDiagBlocksLowerTriangular" | custom-call | tf_op jit(solution)/shard_map/vmap(jit(_solve_triangular))/triangular_solve | solution.py:48
  811.2 49.8 %all-gather.41.cloned.1.call-done = f32[16,512,256]{2,1,0:T(8,128)} async-done(((f32[2,512,256]{2,1,0:T(8,128)}), f32[16,512,256]{2,1,0:T(8,128)}) %all-gather.41.cloned.1.call-update) | async-done | bytes 8388624 | tf_op jit(solution)/shard_map/all_gather | solution.py:14
  874.6 197.5 %all-gather.43.cloned.1.call-done = f32[32,1024,256]{2,1,0:T(8,128)} async-done(((f32[2,1024,256]{2,1,0:T(8,128)}), f32[32,1024,256]{2,1,0:T(8,128)}) %all-gather.43.cloned.1.call-update) | async-done | bytes 33554448 | tf_op jit(solution)/shard_map/all_gather | solution.py:14
  1072.1 12.1 reduce_sum.145
  1085.8 31.8 %all-gather.45.cloned.1.call-done = f32[16,256,256]{2,1,0:T(8,128)} async-done(((f32[2,256,256]{2,1,0:T(8,128)}), f32[16,256,256]{2,1,0:T(8,128)}) %all-gather.45.cloned.1.call-update) | async-done | bytes 4194320 | tf_op jit(solution)/shard_map/all_gather | solution.py:14
  1120.4 23.6 custom-call.70
  1144.1 19.7 custom-call.71
  1164.5 23.5 custom-call.72
  1192.6 39.5 %custom-call.73 = f32[2,2,128,128]{2,3,1,0:T(8,128)S(1)} custom-call(f32[2,2,128,128]{3,2,1,0:T(8,128)S(1)} %bitcast.434), custom_call_target="InvertDiagBlocksLowerTriangular" | custom-call | tf_op jit(solution)/shard_map/vmap(jit(_solve_triangular))/triangular_solve | solution.py:48
  1238.7 49.8 %all-gather.47.cloned.1.call-done = f32[16,512,256]{2,1,0:T(8,128)} async-done(((f32[2,512,256]{2,1,0:T(8,128)}), f32[16,512,256]{2,1,0:T(8,128)}) %all-gather.47.cloned.1.call-update) | async-done | bytes 8388624 | tf_op jit(solution)/shard_map/all_gather | solution.py:14
  1302.2 197.5 %all-gather.49.cloned.1.call-done = f32[32,1024,256]{2,1,0:T(8,128)} async-done(((f32[2,1024,256]{2,1,0:T(8,128)}), f32[32,1024,256]{2,1,0:T(8,128)}) %all-gather.49.cloned.1.call-update) | async-done | bytes 33554448 | tf_op jit(solution)/shard_map/all_gather | solution.py:14
  1499.7 12.1 reduce_sum.148
  1517.2 28.0 %all-gather.51.cloned.1.call-done = f32[16,256,256]{2,1,0:T(8,128)} async-done(((f32[2,256,256]{2,1,0:T(8,128)}), f32[16,256,256]{2,1,0:T(8,128)}) %all-gather.51.cloned.1.call-update) | async-done | bytes 4194320 | tf_op jit(solution)/shard_map/all_gather | solution.py:14
  1548.0 23.9 custom-call.74
  1571.9 19.7 custom-call.75
  1592.3 23.5 custom-call.76
  1620.2 39.5 %custom-call.77 = f32[2,2,128,128]{2,3,1,0:T(8,128)S(1)} custom-call(f32[2,2,128,128]{3,2,1,0:T(8,128)S(1)} %bitcast.435), custom_call_target="InvertDiagBlocksLowerTriangular" | custom-call | tf_op jit(solution)/shard_map/vmap(jit(_solve_triangular))/triangular_solve | solution.py:48
  1680.3 10.8 gather_fusion.4
  1702.8 13.4 all-gather.53.cloned.1.call-done
  1732.8 35.6 %gather_fusion.6 = f32[2048,512]{1,0:T(8,128)} fusion(f32[2,1024,512]{2,1,0:T(8,128)} %copy.494, s32[2048]{0:T(1024)S(1)} %bitcast.399), kind=kCustom, calls=%fused_computation.6 | custom fusion | bytes 8404992 | tf_op jit(solution)/shard_map/vmap(jit(_take))/gather | solution.py:22
  1778.9 21.3 gather_fusion.7
  1806.8 9.3 all-to-all-start
  1816.5 17.7 gather_fusion.5
  1892.4 85.6 %gather_fusion.8 = f32[3072,512]{1,0:T(8,128)} fusion(f32[2,1025,512]{2,0,1:T(2,128)} %concatenate.19, s32[3072]{0:T(1024)S(1)} %reshape.1288), kind=kCustom, calls=%fused_computation.8 | custom fusion | bytes 12607488 | tf_op jit(solution)/shard_map/vmap(jit(_take))/gather | solution.py:22
  1978.1 10.4 copy.499
  2004.2 51.1 %gather_fusion.9 = f32[1536,1536]{1,0:T(8,128)} fusion(f32[2,513,1536]{2,0,1:T(2,128)} %concatenate.20, s32[1536]{0:T(1024)S(1)} %reshape.1294), kind=kCustom, calls=%fused_computation.9 | custom fusion | bytes 18886656 | tf_op jit(solution)/shard_map/vmap(jit(_take))/gather | solution.py:22
  2055.3 9.7 copy.500
  2077.6 151.6 %all-gather.55.cloned.1.call-done = f32[16,1536,256]{2,1,0:T(8,128)} async-done(((f32[1,1536,256]{2,1,0:T(8,128)}), f32[16,1536,256]{2,1,0:T(8,128)}) %all-gather.55.cloned.1.call-update) | async-done | bytes 25165840 | tf_op jit(solution)/shard_map/all_gather | solution.py:14
  2239.7 24.6 %all-gather.57.cloned.1.call-done = f32[8,256,256]{2,1,0:T(8,128)} async-done(((f32[1,256,256]{2,1,0:T(8,128)}), f32[8,256,256]{2,1,0:T(8,128)}) %all-gather.57.cloned.1.call-update) | async-done | bytes 2097168 | tf_op jit(solution)/shard_map/all_gather | solution.py:14
  2266.4 11.7 custom-call.30
  2278.2 9.8 custom-call.31
  2289.5 11.7 custom-call.32
  2309.5 20.5 custom-call.33
  2338.8 38.7 %all-gather.59.cloned.1.call-done = f32[6144,256]{0,1:T(8,128)} async-done(((f32[768,256]{0,1:T(8,128)}), f32[6144,256]{0,1:T(8,128)}) %all-gather.59.cloned.1.call-update) | async-done | bytes 6291472 | tf_op jit(solution)/shard_map/all_gather | solution.py:14
  (399 shorter events, 330.8 us)
Async XLA Ops:
  8.0 208.9 %all-gather.31.cloned.1.call-start = ((), (), s32[]{:S(2)}) async-start(), calls=%async_computation.1 | async-start | bytes 35651584 | tf_op jit(solution)/shard_map/all_gather | solution.py:14
  17.0 245.3 %all-gather.33.cloned.1.call-start = ((), (), s32[]{:S(2)}) async-start(), calls=%async_computation.2 | async-start | bytes 4718592 | tf_op jit(solution)/shard_map/all_gather | solution.py:14
  229.0 35.9 %copy-start.10 = (f32[2,1024,256]{2,1,0:T(8,128)}, f32[2,1024,256]{2,1,0:T(8,128)S(1)}, u32[]{:S(2)}) copy-start(f32[2,1024,256]{2,1,0:T(8,128)S(1)} %reduce_sum.139) | copy-start | bytes 6291460
  230.5 202.6 %all-gather.35.cloned.1.call-start = ((), (), s32[]{:S(2)}) async-start(), calls=%async_computation.3 | async-start | bytes 9437184 | tf_op jit(solution)/shard_map/all_gather | solution.py:14
  381.4 55.7 %copy-start.4 = (f32[2,1024,256]{1,2,0:T(8,128)}, f32[2,1024,256]{1,2,0:T(8,128)S(1)}, u32[]{:S(2)}) copy-start(f32[2,1024,256]{1,2,0:T(8,128)S(1)} %convolution_select_fusion.4) | copy-start | bytes 6291460
  383.3 261.0 %all-gather.37.cloned.1.call-start = ((), (), s32[]{:S(2)}) async-start(), calls=%async_computation.4 | async-start | bytes 35651584 | tf_op jit(solution)/shard_map/all_gather | solution.py:14
  442.5 2.0 copy-start.2
  446.7 243.0 %all-gather.39.cloned.1.call-start = ((), (), s32[]{:S(2)}) async-start(), calls=%async_computation.5 | async-start | bytes 4718592 | tf_op jit(solution)/shard_map/all_gather | solution.py:14
  656.3 35.9 %copy-start.11 = (f32[2,1024,256]{2,1,0:T(8,128)}, f32[2,1024,256]{2,1,0:T(8,128)S(1)}, u32[]{:S(2)}) copy-start(f32[2,1024,256]{2,1,0:T(8,128)S(1)} %reduce_sum.142) | copy-start | bytes 6291460
  657.8 203.1 %all-gather.41.cloned.1.call-start = ((), (), s32[]{:S(2)}) async-start(), calls=%async_computation.6 | async-start | bytes 9437184 | tf_op jit(solution)/shard_map/all_gather | solution.py:14
  809.3 55.8 %copy-start.6 = (f32[2,1024,256]{1,2,0:T(8,128)}, f32[2,1024,256]{1,2,0:T(8,128)S(1)}, u32[]{:S(2)}) copy-start(f32[2,1024,256]{1,2,0:T(8,128)S(1)} %convolution_select_fusion.3) | copy-start | bytes 6291460
  811.1 261.0 %all-gather.43.cloned.1.call-start = ((), (), s32[]{:S(2)}) async-start(), calls=%async_computation.7 | async-start | bytes 35651584 | tf_op jit(solution)/shard_map/all_gather | solution.py:14
  870.4 2.0 copy-start.3
  874.6 243.0 %all-gather.45.cloned.1.call-start = ((), (), s32[]{:S(2)}) async-start(), calls=%async_computation.8 | async-start | bytes 4718592 | tf_op jit(solution)/shard_map/all_gather | solution.py:14
  1084.2 35.9 %copy-start.12 = (f32[2,1024,256]{2,1,0:T(8,128)}, f32[2,1024,256]{2,1,0:T(8,128)S(1)}, u32[]{:S(2)}) copy-start(f32[2,1024,256]{2,1,0:T(8,128)S(1)} %reduce_sum.145) | copy-start | bytes 6291460
  1085.7 202.8 %all-gather.47.cloned.1.call-start = ((), (), s32[]{:S(2)}) async-start(), calls=%async_computation.9 | async-start | bytes 9437184 | tf_op jit(solution)/shard_map/all_gather | solution.py:14
  1236.9 55.7 %copy-start.7 = (f32[2,1024,256]{1,2,0:T(8,128)}, f32[2,1024,256]{1,2,0:T(8,128)S(1)}, u32[]{:S(2)}) copy-start(f32[2,1024,256]{1,2,0:T(8,128)S(1)} %convolution_select_fusion.2) | copy-start | bytes 6291460
  1238.7 261.0 %all-gather.49.cloned.1.call-start = ((), (), s32[]{:S(2)}) async-start(), calls=%async_computation.10 | async-start | bytes 35651584 | tf_op jit(solution)/shard_map/all_gather | solution.py:14
  1298.0 2.0 copy-start.1
  1302.1 243.0 %all-gather.51.cloned.1.call-start = ((), (), s32[]{:S(2)}) async-start(), calls=%async_computation.11 | async-start | bytes 4718592 | tf_op jit(solution)/shard_map/all_gather | solution.py:14
  1511.8 1.6 copy-start.9
  1513.3 159.5 %sort.39.cloned.1.call-start = ((), (), s32[]{:S(2)}) async-start(), calls=%async_computation.17 | async-start | bytes 393248 | tf_op jit(solution)/shard_map/jit(argsort)/sort | solution.py:93
  1515.8 175.6 %sort.37.cloned.1.call-start = ((), (), s32[]{:S(2)}) async-start(), calls=%async_computation.16 | async-start | bytes 393248 | tf_op jit(solution)/shard_map/jit(argsort)/sort | solution.py:94
  1517.1 199.1 %all-gather.53.cloned.1.call-start = ((), (), s32[]{:S(2)}) async-start(), calls=%async_computation.12 | async-start | bytes 9437184 | tf_op jit(solution)/shard_map/all_gather | solution.py:14
  1664.6 55.7 %copy-start.8 = (f32[2,1024,256]{1,2,0:T(8,128)}, f32[2,1024,256]{1,2,0:T(8,128)S(1)}, u32[]{:S(2)}) copy-start(f32[2,1024,256]{1,2,0:T(8,128)S(1)} %convolution_select_fusion.1) | copy-start | bytes 6291460
  1778.9 21.4 copy-start.16
  1806.8 60.1 %all-to-all-start = ((f32[128,2,128,32]{2,3,1,0:T(8,128)}), f32[128,2,128,32]{2,3,1,0:T(8,128)}, u32[]{:S(2)}, u32[]{:S(2)}) async-start(f32[128,2,128,32]{2,3,1,0:T(8,128)} %bitcast.416), calls=%async_computation | async-start | bytes 8388608 | tf_op jit(solution)/shard_map/all_to_all | solution.py:127
  1816.1 413.1 %all-gather.55.cloned.1.call-start = ((), (), s32[]{:S(2)}) async-start(), calls=%async_computation.13 | async-start | bytes 26738688 | tf_op jit(solution)/shard_map/all_gather | solution.py:14
  1816.5 17.8 copy-start.19
  1816.5 18.2 copy-start.21
  1834.2 18.4 copy-start.18
  1834.2 18.7 copy-start.20
  2055.3 14.4 slice-start.3
  2064.9 4.9 slice-start.4
  2069.8 5.0 copy-start
  2077.6 186.7 %all-gather.57.cloned.1.call-start = ((), (), s32[]{:S(2)}) async-start(), calls=%async_computation.14 | async-start | bytes 2359296 | tf_op jit(solution)/shard_map/all_gather | solution.py:14
  2238.5 49.7 %copy-start.15 = (f32[1536,256]{1,0:T(8,128)}, f32[1536,256]{1,0:T(8,128)S(1)}, u32[]{:S(2)}) copy-start(f32[1536,256]{1,0:T(8,128)S(1)} %reduce.33) | copy-start | bytes 4718596
  2239.4 138.2 %all-gather.59.cloned.1.call-start = ((), (), s32[]{:S(2)}) async-start(), calls=%async_computation.15 | async-start | bytes 7077888 | tf_op jit(solution)/shard_map/all_gather | solution.py:14
  2266.4 21.8 copy-start.17
  2288.2 48.0 %copy-start.5 = (f32[2,1024,256]{1,2,0:T(8,128)S(1)}, f32[2,1024,256]{1,2,0:T(8,128)}, u32[]{:S(2)}) copy-start(f32[2,1024,256]{1,2,0:T(8,128)} %copy-done.4) | copy-start | bytes 6291460
  2333.8 1.1 copy-start.13
  2336.2 48.5 %slice-start = ((s8[9437184]{0:T(1024)(128)(4,1)}), s8[1048576]{0:T(1024)(128)(4,1)S(1)}, s32[]{:S(2)}) async-start(s8[9437184]{0:T(1024)(128)(4,1)} %bitcast.403), calls=%async_computation.20 | async-start | bytes 2097152
  2377.5 7.1 slice-start.1
  2377.5 7.1 slice-start.2
  2383.1 1.6 copy-start.14
Sparse Core Ops, SparseCore 0:
  17.2 199.6 all-gather.30
  230.6 31.7 all-gather.32
  383.4 49.6 all-gather.34
  446.8 197.3 all-gather.36
  658.0 31.7 all-gather.38
  811.3 49.6 all-gather.40
  874.7 197.3 all-gather.42
  1085.8 31.7 all-gather.44
  1238.8 49.6 all-gather.46
  1302.3 197.3 all-gather.48
  1513.4 31.7 all-gather.50
  1666.5 49.6 all-gather.52
  2077.7 151.4 all-gather.54
  2239.5 24.7 all-gather.56
  2336.3 41.2 all-gather.58
Sparse Core Ops, SparseCore 1:
  1516.8 7.0 sort.43.cloned.1.call-done
  1526.3 9.7 sort.41.cloned.1.call-done
  (2 shorter events, 0.0 us)
